TPU v7x, 32 devices: a whole 2x2x4 slice. The times are simulated.
32 devices in a mesh: sec: 4 (over x, core), sub: 8 (over z, y).
Axes of the slice: x: 2, y: 2, z: 4, core: 2. Of those that a mesh axis runs over, the one named last changes fastest.
Arguments:
- schur: bfloat16 [8, 1024, 1024], P('sub', 'sec'), may hold values from -0.1875 to 0.1875
- neumann: bfloat16 [8, 1024, 1024], P('sub', 'sec'), may hold values from -0.1875 to 0.1875
- constraint_weights: bfloat16 [8, 1024, 128], P('sub', 'sec'), may hold values from -0.1875 to 0.1875
- coarse_inverse: bfloat16 [8, 768, 768], P('sub', 'sec'), may hold values from -0.21875 to 0.21875
- solution: bfloat16 [8, 1024, 128], P('sub', 'sec'), may hold values from -6 to 6
- load: bfloat16 [8, 1024, 128], P('sub', 'sec'), may hold values from -6 to 6
- neighbours: int32 [8, 4], P('sub'), may hold values from 0 to 7, as said below
- face_index: int32 [8, 1024], P('sub', 'sec'), may hold values from 0 to 255, as said below
- coarse_dof: int32 [8, 128], P('sub'), may hold values from 0 to 6143, as said below
Outputs:
- precond: bfloat16 [8, 1024, 128], P('sub', 'sec')
- image: bfloat16 [8, 1024, 128], P('sub', 'sec')
Inputs may be any that keep to these rules, and one draw needn't show every extreme that they name: `neighbours`: the subdomain glued to face f of subdomain i is another subdomain whose column c // 1 is the column i // 1 of i or the one before or after it, cyclically over 8 columns. `face_index`: for each subdomain and face, the entries of the face's 256 unknowns are a permutation of 0 to 255. `coarse_dof`: constraint k of subdomain i maps to an unknown of the cluster of column i // 1 or of the column before or after it, cyclically. Each cluster has 64 coarse unknowns that are used, and each used unknown is the unknown of exactly two constraints.
All inputs are finite; a program needn't handle non-finite values.
Results may differ from a plain program's by a relative error of at most 0.0058.
Values may be sent and summed in bfloat16 or wider, within the bound.
No kernel may reach another device: no remote copies, remote signals or barrier semaphores. Data moves between devices by JAX's collectives and lax.ppermute only.
A program may use at most 64 MiB of HBM per device.

v0:
```python
import jax
import jax.numpy as jnp
from jax import lax
from jax.sharding import PartitionSpec as P

COLS = 128


def extended(cells, sides, width):
    for axis, dim in sides:
        count = lax.axis_size(axis)
        head = lax.slice_in_dim(cells, 0, width, axis=dim)
        tail = lax.slice_in_dim(cells, cells.shape[dim] - width, cells.shape[dim], axis=dim)
        cells = jnp.concatenate(
            [
                lax.ppermute(tail, axis, [(i, (i + 1) % count) for i in range(count)]),
                cells,
                lax.ppermute(head, axis, [((i + 1) % count, i) for i in range(count)]),
            ],
            axis=dim,
        )
    return cells


def row_folder(blocks, received):
    return jnp.einsum("srk,skc->src", blocks, received, preferred_element_type=jnp.float32)


def face_selector(face_index):
    face_len = face_index.shape[1]
    positions = lax.broadcasted_iota(jnp.int32, (face_index.shape[0], face_len, face_len), 2)
    return (face_index[:, :, None] == positions).astype(jnp.float32)


def pair_faces(own_field, rim_rows, rim_slot, selector):
    matched = jnp.take(rim_rows, rim_slot, axis=0)
    facing = jnp.einsum(
        "sde,sec->sdc",
        selector,
        matched,
        precision=lax.Precision.HIGHEST,
        preferred_element_type=jnp.float32,
    )
    return own_field + facing


def local(
    schur,
    neumann,
    constraint_weights,
    coarse_inverse,
    solution,
    load,
    neighbours,
    face_index,
    coarse_dof,
):
    sub_count = schur.shape[0]
    col_count = COLS
    coarse_len = coarse_inverse.shape[2]
    inverse_rows = coarse_inverse[0]
    my_column = lax.axis_index("sub")
    axis_len = lax.axis_size("sub")
    my_section = lax.axis_index("sec")
    nbr_ids = jnp.take(neighbours, my_section, axis=1)
    rim_slot = (nbr_ids // sub_count - my_column + 1) % axis_len * sub_count + nbr_ids % sub_count
    coarse_slot = (
        coarse_dof // coarse_len - my_column + 1
    ) % axis_len * coarse_len + coarse_dof % coarse_len
    selector = face_selector(face_index)
    dof_near = extended(coarse_dof, (("sub", 0),), sub_count)
    is_owned = dof_near // coarse_len == my_column
    owned_slot = jnp.where(is_owned, dof_near % coarse_len, coarse_len).reshape(-1)
    schur_iter = row_folder(schur, lax.all_gather(solution, "sec", axis=1, tiled=True))
    residual = load.astype(jnp.float32) - schur_iter
    residual_near = extended(residual, (("sub", 0),), sub_count)
    assembled = pair_faces(residual, residual_near, rim_slot, selector).astype(jnp.bfloat16)
    constraint_part = jnp.einsum(
        "srk,src->skc", constraint_weights, assembled, preferred_element_type=jnp.float32
    )
    constraint_values = lax.psum(constraint_part, "sec")
    value_near = extended(constraint_values, (("sub", 0),), sub_count)
    coarse_rhs = jax.ops.segment_sum(
        value_near.reshape(-1, col_count), owned_slot, num_segments=coarse_len + 1
    )[:coarse_len]
    coarse_piece = jnp.dot(
        inverse_rows, coarse_rhs.astype(jnp.bfloat16), preferred_element_type=jnp.float32
    ).astype(jnp.bfloat16)
    coarse_whole = lax.all_gather(coarse_piece, "sec", axis=0, tiled=True)
    coarse_near = extended(coarse_whole, (("sub", 0),), coarse_len)
    picked = jnp.take(coarse_near, coarse_slot.reshape(-1), axis=0).reshape(
        sub_count, -1, col_count
    )
    neumann_part = row_folder(neumann, lax.all_gather(assembled, "sec", axis=1, tiled=True))
    correction = neumann_part + jnp.einsum(
        "srk,skc->src", constraint_weights, picked, preferred_element_type=jnp.float32
    )
    correction_near = extended(correction, (("sub", 0),), sub_count)
    precond = (0.5 * pair_faces(correction, correction_near, rim_slot, selector)).astype(
        jnp.bfloat16
    )
    precond_image = row_folder(schur, lax.all_gather(precond, "sec", axis=1, tiled=True)).astype(
        jnp.bfloat16
    )
    return (precond, precond_image)


def solution(mesh):
    placed = (
        P("sub", "sec", None),
        P("sub", "sec", None),
        P("sub", "sec", None),
        P("sub", "sec", None),
        P("sub", "sec", None),
        P("sub", "sec", None),
        P("sub", None),
        P("sub", "sec"),
        P("sub", None),
    )
    return jax.shard_map(
        local,
        mesh=mesh,
        in_specs=placed,
        out_specs=(P("sub", "sec", None), P("sub", "sec", None)),
        check_vma=False,
    )
```

profile of v0, /device:TPU:0, one launch (start us, length us, event | category | flops | bytes accessed | tf_op | source)
XLA Modules:
  0.0 114.4 jit_solution(5369333689216355976)
XLA Ops:
  7.2 7.6 %all_gather.12 = bf16[1,1024,128]{2,1,0:T(8,128)(2,1)S(1)} all-gather(bf16[1,256,128]{2,1,0:T(8,128)(2,1)} %param.15), channel_id=1, replica_groups=mesh['sec'=4,'sub'=8] {'sec'}, dimensions={1}, use_global_device_ids=true | all-gather | bytes 327680 | tf_op jit(solution)/shard_map/all_gather | solution.py:74
  14.8 1.2 %fusion.2 = f32[1,256,128]{2,1,0:T(8,128)S(1)} fusion(bf16[1,256,1024]{2,1,0:T(8,128)(2,1)S(1)} %copy-done, bf16[1,1024,128]{2,1,0:T(8,128)(2,1)S(1)} %all_gather.12, bf16[1,256,128]{2,1,0:T(8,128)(2,1)} %param.16), kind=kOutput, calls=%fused_computation.8 | convolution fusion | flops 67174400 | bytes 983040 | tf_op jit(solution)/shard_map/srk,skc->src/dot_general | solution.py:26
  16.0 1.6 %collective-permute-start = (f32[1,256,128]{2,1,0:T(8,128)S(1)}, f32[1,256,128]{2,1,0:T(8,128)S(1)}, u32[]{:S(2)}, u32[]{:S(2)}) collective-permute-start(f32[1,256,128]{2,1,0:T(8,128)S(1)} %fusion.2), channel_id=1, source_target_pairs={{0,1},{1,2},{2,3},{3,4},{4,5},{5,6},{6,7},{7,0},{8,9},{9,10},{10,1... | collective-permute-start | bytes 393224 | tf_op jit(solution)/shard_map/ppermute | solution.py:16
  17.6 3.2 %collective-permute-start.1 = (f32[1,256,128]{2,1,0:T(8,128)S(1)}, f32[1,256,128]{2,1,0:T(8,128)S(1)}, u32[]{:S(2)}, u32[]{:S(2)}) collective-permute-start(f32[1,256,128]{2,1,0:T(8,128)S(1)} %fusion.2), channel_id=1, source_target_pairs={{1,0},{2,1},{3,2},{4,3},{5,4},{6,5},{7,6},{0,7},{9,8},{10,9},{11,1... | collective-permute-start | bytes 393224 | tf_op jit(solution)/shard_map/ppermute | solution.py:18
  20.8 4.7 %collective-permute-start.3 = (s32[1,128]{1,0:T(1,128)S(1)}, s32[1,128]{1,0:T(1,128)S(1)}, u32[]{:S(2)}, u32[]{:S(2)}) collective-permute-start(s32[1,128]{1,0:T(1,128)S(1)} %copy-done.4), channel_id=1, source_target_pairs={{1,0},{2,1},{3,2},{4,3},{5,4},{6,5},{7,6},{0,7},{9,8},{10,9},{11,1... | collective-permute-start | bytes 1544 | tf_op jit(solution)/shard_map/ppermute | solution.py:18
  25.5 0.6 constant_dynamic-slice_fusion
  27.1 0.3 fusion.4
  27.4 0.8 convolution_bitcast_fusion.2
  28.3 33.1 %all-reduce.2.cloned.1.call-done = f32[1,128,128]{1,2,0:T(8,128)} async-done(((f32[1,128,128]{1,2,0:T(8,128)}), f32[1,128,128]{1,2,0:T(8,128)}) %all-reduce.2.cloned.1.call-update) | async-done | bytes 65552 | tf_op jit(solution)/shard_map/psum | solution.py:81
  61.4 1.5 %collective-permute-start.4 = (f32[1,128,128]{1,2,0:T(8,128)}, f32[1,128,128]{1,2,0:T(8,128)S(1)}, u32[]{:S(2)}, u32[]{:S(2)}) collective-permute-start(f32[1,128,128]{1,2,0:T(8,128)} %all-reduce.2.cloned.1.call-done), channel_id=1, source_target_pairs={{0,1},{1,2},{2,3},{3,4},{4,5},{5,6},{6,7},{7,0},{8,9},{9,10},{10,1... | collective-permute-start | bytes 196616 | tf_op jit(solution)/shard_map/ppermute | solution.py:16
  62.9 3.2 %collective-permute-start.5 = (f32[1,128,128]{1,2,0:T(8,128)}, f32[1,128,128]{1,2,0:T(8,128)S(1)}, u32[]{:S(2)}, u32[]{:S(2)}) collective-permute-start(f32[1,128,128]{1,2,0:T(8,128)} %all-reduce.2.cloned.1.call-done), channel_id=1, source_target_pairs={{1,0},{2,1},{3,2},{4,3},{5,4},{6,5},{7,6},{0,7},{9,8},{10,9},{11,1... | collective-permute-start | bytes 196616 | tf_op jit(solution)/shard_map/ppermute | solution.py:18
  66.2 2.4 %collective-permute-done.4 = f32[1,128,128]{1,2,0:T(8,128)S(1)} collective-permute-done((f32[1,128,128]{1,2,0:T(8,128)}, f32[1,128,128]{1,2,0:T(8,128)S(1)}, u32[]{:S(2)}, u32[]{:S(2)}) %collective-permute-start.4) | collective-permute-done | bytes 65568 | tf_op jit(solution)/shard_map/ppermute | solution.py:16
  68.6 0.9 pad_maximum_fusion.1
  69.6 2.5 %scatter_custom_fusion = f32[769,128]{1,0:T(8,128)S(1)} fusion(s32[384]{0:T(512)S(1)} %fusion.45, f32[384,128]{1,0:T(8,128)S(1)} %bitcast.118, f32[]{:T(128)} %constant.133.clone.1), kind=kCustom, calls=%fused_computation.32 | custom fusion | flops 49152 | bytes 393732 | tf_op jit(solution)/shard_map/scatter-add | solution.py:83
  72.0 0.2 fusion.6
  72.3 5.6 %all_gather.14 = bf16[768,128]{1,0:T(8,128)(2,1)S(1)} all-gather(bf16[192,128]{1,0:T(8,128)(2,1)S(1)} %fusion.6), channel_id=1, replica_groups=mesh['sec'=4,'sub'=8] {'sec'}, dimensions={0}, use_global_device_ids=true | all-gather | bytes 245760 | tf_op jit(solution)/shard_map/all_gather | solution.py:89
  77.9 1.1 collective-permute-start.6
  79.0 3.6 %collective-permute-start.7 = (bf16[768,128]{1,0:T(8,128)(2,1)S(1)}, bf16[768,128]{1,0:T(8,128)(2,1)S(1)}, u32[]{:S(2)}, u32[]{:S(2)}) collective-permute-start(bf16[768,128]{1,0:T(8,128)(2,1)S(1)} %all_gather.14), channel_id=1, source_target_pairs={{1,0},{2,1},{3,2},{4,3},{5,4},{6,5},{7,6},{0,7},{9,8},{10,9},{11,1... | collective-permute-start | bytes 589832 | tf_op jit(solution)/shard_map/ppermute | solution.py:18
  82.6 5.8 %all_gather.13 = bf16[1,1024,128]{2,1,0:T(8,128)(2,1)S(1)} all-gather(bf16[1,256,128]{2,1,0:T(8,128)(2,1)S(1)} %fusion.4), channel_id=1, replica_groups=mesh['sec'=4,'sub'=8] {'sec'}, dimensions={1}, use_global_device_ids=true | all-gather | bytes 327680 | tf_op jit(solution)/shard_map/all_gather | solution.py:94
  88.4 1.7 %collective-permute-done.7 = bf16[768,128]{1,0:T(8,128)(2,1)S(1)} collective-permute-done((bf16[768,128]{1,0:T(8,128)(2,1)S(1)}, bf16[768,128]{1,0:T(8,128)(2,1)S(1)}, u32[]{:S(2)}, u32[]{:S(2)}) %collective-permute-start.7) | collective-permute-done | bytes 196640 | tf_op jit(solution)/shard_map/ppermute | solution.py:18
  90.1 0.7 gather_fusion
  90.8 0.3 fusion.30
  91.1 0.3 convolution_add_fusion
  91.4 0.3 collective-permute-start.8
  91.8 4.4 %collective-permute-start.9 = (f32[1,256,128]{1,2,0:T(8,128)S(1)}, f32[1,256,128]{1,2,0:T(8,128)S(1)}, u32[]{:S(2)}, u32[]{:S(2)}) collective-permute-start(f32[1,256,128]{1,2,0:T(8,128)S(1)} %bitcast.115), channel_id=1, source_target_pairs={{1,0},{2,1},{3,2},{4,3},{5,4},{6,5},{7,6},{0,7},{9,8},{10,9},{11,1... | collective-permute-start | bytes 393224 | tf_op jit(solution)/shard_map/ppermute | solution.py:18
  96.2 2.9 %collective-permute-done.8 = f32[1,256,128]{1,2,0:T(8,128)S(1)} collective-permute-done((f32[1,256,128]{1,2,0:T(8,128)S(1)}, f32[1,256,128]{1,2,0:T(8,128)S(1)}, u32[]{:S(2)}, u32[]{:S(2)}) %collective-permute-start.8) | collective-permute-done | bytes 131104 | tf_op jit(solution)/shard_map/ppermute | solution.py:16
  99.1 0.5 collective-permute-done.9
  99.6 0.4 fusion.3
  100.0 5.8 %all-gather = bf16[1024,128]{0,1:T(8,128)(2,1)S(1)} all-gather(bf16[256,128]{0,1:T(8,128)(2,1)S(1)} %fusion.3), channel_id=2, replica_groups=mesh['sec'=4,'sub'=8] {'sec'}, dimensions={0}, use_global_device_ids=true | all-gather | bytes 327680 | tf_op jit(solution)/shard_map/all_gather | solution.py:102
  105.8 0.3 fusion.5
  106.1 0.7 copy.17
  106.8 0.7 copy.16
  (31 shorter events, 0.6 us)
Async XLA Ops:
  7.2 7.6 %copy-start = (bf16[1,256,1024]{2,1,0:T(8,128)(2,1)S(1)}, bf16[1,256,1024]{2,1,0:T(8,128)(2,1)}, u32[]{:S(2)}) copy-start(bf16[1,256,1024]{2,1,0:T(8,128)(2,1)} %param.11) | copy-start | bytes 1572868
  7.2 13.6 %copy-start.4 = (s32[1,128]{1,0:T(1,128)S(1)}, s32[1,128]{1,0:T(1,128)}, u32[]{:S(2)}) copy-start(s32[1,128]{1,0:T(1,128)} %param.19) | copy-start | bytes 1540
  7.2 18.3 %copy-start.6 = (s32[1,4]{1,0:T(1,128)S(1)}, s32[1,4]{1,0:T(1,128)}, u32[]{:S(2)}) copy-start(s32[1,4]{1,0:T(1,128)} %param.17) | copy-start | bytes 52
  7.2 54.2 %all-reduce.2.cloned.1.call-start = ((), (), s32[]{:S(2)}) async-start(), calls=%async_computation | async-start | bytes 131072 | tf_op jit(solution)/shard_map/psum | solution.py:81
  14.8 12.3 %copy-start.5 = (s32[1,256]{1,0:T(1,128)S(1)}, s32[1,256]{1,0:T(1,128)}, u32[]{:S(2)}) copy-start(s32[1,256]{1,0:T(1,128)} %param.18) | copy-start | bytes 3076
  14.8 12.6 %copy-start.3 = (bf16[1,256,128]{2,1,0:T(8,128)(2,1)S(1)}, bf16[1,256,128]{2,1,0:T(8,128)(2,1)}, u32[]{:S(2)}) copy-start(bf16[1,256,128]{2,1,0:T(8,128)(2,1)} %param.13) | copy-start | bytes 196612
  16.0 11.1 %collective-permute-start = (f32[1,256,128]{2,1,0:T(8,128)S(1)}, f32[1,256,128]{2,1,0:T(8,128)S(1)}, u32[]{:S(2)}, u32[]{:S(2)}) collective-permute-start(f32[1,256,128]{2,1,0:T(8,128)S(1)} %fusion.2), channel_id=1, source_target_pairs={{0,1},{1,2},{2,3},{3,4},{4,5},{5,6},{6,7},{7,0},{8,9},{9,10},{10,1... | collective-permute-start | bytes 393224 | tf_op jit(solution)/shard_map/ppermute | solution.py:16
  17.6 9.5 %collective-permute-start.1 = (f32[1,256,128]{2,1,0:T(8,128)S(1)}, f32[1,256,128]{2,1,0:T(8,128)S(1)}, u32[]{:S(2)}, u32[]{:S(2)}) collective-permute-start(f32[1,256,128]{2,1,0:T(8,128)S(1)} %fusion.2), channel_id=1, source_target_pairs={{1,0},{2,1},{3,2},{4,3},{5,4},{6,5},{7,6},{0,7},{9,8},{10,9},{11,1... | collective-permute-start | bytes 393224 | tf_op jit(solution)/shard_map/ppermute | solution.py:18
  20.8 6.3 %collective-permute-start.2 = (s32[1,128]{1,0:T(1,128)S(1)}, s32[1,128]{1,0:T(1,128)S(1)}, u32[]{:S(2)}, u32[]{:S(2)}) collective-permute-start(s32[1,128]{1,0:T(1,128)S(1)} %copy-done.4), channel_id=1, source_target_pairs={{0,1},{1,2},{2,3},{3,4},{4,5},{5,6},{6,7},{7,0},{8,9},{9,10},{10,1... | collective-permute-start | bytes 1544 | tf_op jit(solution)/shard_map/ppermute | solution.py:16
  20.8 6.3 %collective-permute-start.3 = (s32[1,128]{1,0:T(1,128)S(1)}, s32[1,128]{1,0:T(1,128)S(1)}, u32[]{:S(2)}, u32[]{:S(2)}) collective-permute-start(s32[1,128]{1,0:T(1,128)S(1)} %copy-done.4), channel_id=1, source_target_pairs={{1,0},{2,1},{3,2},{4,3},{5,4},{6,5},{7,6},{0,7},{9,8},{10,9},{11,1... | collective-permute-start | bytes 1544 | tf_op jit(solution)/shard_map/ppermute | solution.py:18
  61.4 7.2 %collective-permute-start.4 = (f32[1,128,128]{1,2,0:T(8,128)}, f32[1,128,128]{1,2,0:T(8,128)S(1)}, u32[]{:S(2)}, u32[]{:S(2)}) collective-permute-start(f32[1,128,128]{1,2,0:T(8,128)} %all-reduce.2.cloned.1.call-done), channel_id=1, source_target_pairs={{0,1},{1,2},{2,3},{3,4},{4,5},{5,6},{6,7},{7,0},{8,9},{9,10},{10,1... | collective-permute-start | bytes 196616 | tf_op jit(solution)/shard_map/ppermute | solution.py:16
  62.9 5.7 %collective-permute-start.5 = (f32[1,128,128]{1,2,0:T(8,128)}, f32[1,128,128]{1,2,0:T(8,128)S(1)}, u32[]{:S(2)}, u32[]{:S(2)}) collective-permute-start(f32[1,128,128]{1,2,0:T(8,128)} %all-reduce.2.cloned.1.call-done), channel_id=1, source_target_pairs={{1,0},{2,1},{3,2},{4,3},{5,4},{6,5},{7,6},{0,7},{9,8},{10,9},{11,1... | collective-permute-start | bytes 196616 | tf_op jit(solution)/shard_map/ppermute | solution.py:18
  66.1 5.9 %copy-start.2 = (bf16[1,192,768]{2,1,0:T(8,128)(2,1)S(1)}, bf16[1,192,768]{2,1,0:T(8,128)(2,1)}, u32[]{:S(2)}) copy-start(bf16[1,192,768]{2,1,0:T(8,128)(2,1)} %param.14) | copy-start | bytes 884740
  77.9 10.5 %collective-permute-start.6 = (bf16[768,128]{1,0:T(8,128)(2,1)S(1)}, bf16[768,128]{1,0:T(8,128)(2,1)S(1)}, u32[]{:S(2)}, u32[]{:S(2)}) collective-permute-start(bf16[768,128]{1,0:T(8,128)(2,1)S(1)} %all_gather.14), channel_id=1, source_target_pairs={{0,1},{1,2},{2,3},{3,4},{4,5},{5,6},{6,7},{7,0},{8,9},{9,10},{10,1... | collective-permute-start | bytes 589832 | tf_op jit(solution)/shard_map/ppermute | solution.py:16
  79.0 11.1 %collective-permute-start.7 = (bf16[768,128]{1,0:T(8,128)(2,1)S(1)}, bf16[768,128]{1,0:T(8,128)(2,1)S(1)}, u32[]{:S(2)}, u32[]{:S(2)}) collective-permute-start(bf16[768,128]{1,0:T(8,128)(2,1)S(1)} %all_gather.14), channel_id=1, source_target_pairs={{1,0},{2,1},{3,2},{4,3},{5,4},{6,5},{7,6},{0,7},{9,8},{10,9},{11,1... | collective-permute-start | bytes 589832 | tf_op jit(solution)/shard_map/ppermute | solution.py:18
  88.4 2.7 %copy-start.1 = (bf16[1,256,1024]{2,1,0:T(8,128)(2,1)S(1)}, bf16[1,256,1024]{2,1,0:T(8,128)(2,1)}, u32[]{:S(2)}) copy-start(bf16[1,256,1024]{2,1,0:T(8,128)(2,1)} %param.12) | copy-start | bytes 1572868
  91.4 7.7 %collective-permute-start.8 = (f32[1,256,128]{1,2,0:T(8,128)S(1)}, f32[1,256,128]{1,2,0:T(8,128)S(1)}, u32[]{:S(2)}, u32[]{:S(2)}) collective-permute-start(f32[1,256,128]{1,2,0:T(8,128)S(1)} %bitcast.114), channel_id=1, source_target_pairs={{0,1},{1,2},{2,3},{3,4},{4,5},{5,6},{6,7},{7,0},{8,9},{9,10},{10,1... | collective-permute-start | bytes 393224 | tf_op jit(solution)/shard_map/ppermute | solution.py:16
  91.8 7.8 %collective-permute-start.9 = (f32[1,256,128]{1,2,0:T(8,128)S(1)}, f32[1,256,128]{1,2,0:T(8,128)S(1)}, u32[]{:S(2)}, u32[]{:S(2)}) collective-permute-start(f32[1,256,128]{1,2,0:T(8,128)S(1)} %bitcast.115), channel_id=1, source_target_pairs={{1,0},{2,1},{3,2},{4,3},{5,4},{6,5},{7,6},{0,7},{9,8},{10,9},{11,1... | collective-permute-start | bytes 393224 | tf_op jit(solution)/shard_map/ppermute | solution.py:18
Sparse Core Ops, SparseCore 0:
  28.4 32.9 all-reduce.1
where the time goes:
time: 115 us; the launch traced here: 114 us
  waiting for transfers between devices  40.9 us (36%)
  blocking collectives  24.7 us (21%)
  starting transfers between devices  23.8 us (21%)
  between operations  14.9 us (13%)
  matrix products  3.78 us (3%)
  other arithmetic  3.46 us (3%)
  local copies, waits for them, and re-layouts  2.92 us (3%)
    psum x1, waiting for transfers between devices, local(): constraint_values = lax.psum(constraint_part, 'sec')  33.1 us
    ppermute x5, starting transfers between devices, extended(): lax.ppermute(head, axis, [((i + 1) % count, i) for i in range(count)])  19.2 us
    all_gather x1, blocking collectives, local(): lax.all_gather(solution, 'sec', axis=1, tiled=True)  7.57 us
    all_gather x1, blocking collectives, local(): lax.all_gather(precond, 'sec', axis=1, tiled=True)  5.78 us
    all_gather x1, blocking collectives, local(): lax.all_gather(assembled, 'sec', axis=1, tiled=True)  5.76 us
    all_gather x1, blocking collectives, local(): coarse_whole = lax.all_gather(coarse_piece, 'sec', axis=0, tiled=True)  5.6 us
    ppermute x5, waiting for transfers between devices, extended(): lax.ppermute(tail, axis, [(i, (i + 1) % count) for i in range(count)])  5.58 us
    ppermute x5, starting transfers between devices, extended(): lax.ppermute(tail, axis, [(i, (i + 1) % count) for i in range(count)])  4.53 us
  transfers between devices with their start and end apart: 11, of which 6 were waited for; matrix products, arithmetic and copies ran while one was open for 1% of the time, Pallas kernels for 0%

commit v1 on v0

v1 whole, which is shorter than its diff:
```python
import jax
import jax.numpy as jnp
from jax import lax
from jax.sharding import PartitionSpec as P

F32 = jnp.float32
BF16 = jnp.bfloat16
KINDS = ("A2", "B2", "A3", "B3")


def partner(kind, i, count):
    forward = {
        "A": i % 2 == 0,
        "B": i % 2 == 1,
        "A2": i % 4 < 2,
        "B2": i % 4 >= 2,
        "A3": i % 2 == 0,
        "B3": i % 2 == 1,
    }[kind]
    step = {"2": 2, "3": 3}.get(kind[-1], 1)
    return (i + step if forward else i - step) % count


def swap_columns(array, kind):
    count = lax.axis_size("sub")
    return lax.ppermute(array, "sub", [(i, partner(kind, i, count)) for i in range(count)])


def swap_by_section(array, kinds):
    sections, count = lax.axis_size("sec"), lax.axis_size("sub")
    moves = [
        (s * count + i, s * count + partner(kinds[s % len(kinds)], i, count))
        for s in range(sections)
        for i in range(count)
    ]
    return lax.ppermute(array, ("sec", "sub"), moves)


def swap_cores(array):
    return lax.ppermute(array, "sec", [(i, i ^ 1) for i in range(lax.axis_size("sec"))])


def dot(a, b):
    return jnp.dot(a, b, preferred_element_type=F32)


def encode_dof(dof, column, count, coarse_len):
    near = (dof // coarse_len - column + 1) % count
    slot = dof % coarse_len
    parts = -(-coarse_len // 128)
    rows = jnp.stack([near * parts + slot // 128, slot % 128]).astype(BF16)
    return jnp.pad(rows, ((0, 14), (0, 0)))


def decode_dof(rows, offset, coarse_len):
    parts = -(-coarse_len // 128)
    whole = rows[:2].astype(F32).astype(jnp.int32)
    cluster = offset + 1 + whole[0] // parts
    return cluster, whole[0] % parts * 128 + whole[1]


def local(
    schur,
    neumann,
    constraint_weights,
    coarse_inverse,
    solution,
    load,
    neighbours,
    face_index,
    coarse_dof,
):
    s_rows, n_rows, weights = schur[0], neumann[0], constraint_weights[0]
    c_rows = coarse_inverse[0]
    face_len, cons = weights.shape
    coarse_part, coarse_len = c_rows.shape
    used = cons // 2
    column, section = lax.axis_index("sub"), lax.axis_index("sec")
    count = lax.axis_size("sub")
    core = section % 2

    even = column % 2 == 0
    off1 = jnp.where(even, 1, -1)
    off2 = jnp.where(column % 4 < 2, 2, -2)
    off3 = jnp.where(even, 3, -3)

    own_code = encode_dof(coarse_dof[0], column, count, coarse_len)
    far_code = swap_by_section(own_code, KINDS)
    first = jnp.concatenate([weights, own_code])
    near_b = swap_columns(first, "B")
    near_a = swap_columns(first, "A")

    iterate = lax.all_gather(solution[0], "sec", axis=0, tiled=True)
    residual = load[0].astype(F32) - dot(s_rows, iterate)

    residual_half = residual.astype(BF16)
    res_b = swap_columns(residual_half, "B")
    res_a = swap_columns(residual_half, "A")

    nbr = neighbours[0, section]
    want_a = ((nbr - column - off1) % count) == 0
    positions = lax.broadcasted_iota(jnp.int32, (face_len, face_len), 1)
    selector = (face_index[0][:, None] == positions).astype(BF16)

    dec = lambda rows, off: decode_dof(rows, off, coarse_len)
    parts3 = [
        dec(own_code, 0),
        dec(near_a[face_len:], off1),
        dec(near_b[face_len:], -off1),
    ]
    clus3 = jnp.concatenate([p[0] for p in parts3])
    slot3 = jnp.concatenate([p[1] for p in parts3])
    key3 = jnp.where(clus3 == 2, slot3, -1)
    less = (key3[None, :] >= 0) & (key3[None, :] < key3[:, None])
    rank3 = jnp.where(key3 >= 0, jnp.sum(less.astype(jnp.int32), axis=1) // 2, -1)
    by_rank = (lax.broadcasted_iota(jnp.int32, (used, 3 * cons), 0) == rank3[None, :]).astype(BF16)
    by_slot = (key3[:, None] == lax.broadcasted_iota(jnp.int32, (3 * cons, coarse_len), 1)).astype(BF16)
    pick_used = dot(by_rank, by_slot).astype(BF16)
    used_cols = lax.dot_general(
        c_rows, pick_used, (((1,), (1,)), ((), ())), preferred_element_type=F32
    ).astype(BF16)
    pick_rows = lax.dynamic_slice_in_dim(pick_used, section * coarse_part, coarse_part, axis=1)
    used_part = (0.25 * dot(pick_rows, used_cols)).astype(BF16)
    used_part = jnp.pad(used_part, ((0, 0), (0, cons - used)))

    matched = jnp.where(want_a, res_a, res_b)
    assembled = (residual + dot(selector, matched)).astype(BF16)
    values_part = lax.dot_general(
        weights, assembled, (((0,), (0,)), ((), ())), preferred_element_type=F32
    ).astype(BF16)

    packed = jnp.concatenate([assembled, values_part, used_part, far_code])
    around = lax.all_gather(packed, "sec", axis=0)
    assembled_all = around[:, :face_len].reshape(-1, around.shape[2])
    values = jnp.sum(around[:, face_len : face_len + cons].astype(F32), axis=0).astype(BF16)
    at = face_len + cons
    used_block = jnp.sum(around[:, at : at + used].astype(F32), axis=0).astype(BF16)
    far_codes = around[:, at + used :]
    correction = dot(n_rows, assembled_all)

    coarse_load = jnp.concatenate([values, used_block])
    out = jnp.concatenate([correction.astype(BF16), coarse_load])
    far2_mine = swap_by_section(coarse_load, KINDS[:2])
    far3_mine = swap_by_section(values, KINDS[2:])
    cor_b = swap_columns(out, "B")
    cor_a = swap_columns(out, "A")
    far_mine = jnp.concatenate([far2_mine, far3_mine])
    far_other = swap_cores(far_mine)

    sign = jnp.where(core == 0, 1, -1)
    c0 = lambda x, y: jnp.where(core == 0, x, y)
    window = parts3 + [
        dec(c0(far_codes[0], far_codes[1]), sign * off2),
        dec(c0(far_codes[1], far_codes[0]), -sign * off2),
        dec(c0(far_codes[2], far_codes[3]), sign * off3),
        dec(c0(far_codes[3], far_codes[2]), -sign * off3),
    ]
    clus = jnp.concatenate([p[0] for p in window])
    slot = jnp.concatenate([p[1] for p in window])
    inside = (clus >= 0) & (clus < 5)
    same_less = (clus[None, :] == clus[:, None]) & (slot[None, :] < slot[:, None])
    rank = jnp.sum(same_less.astype(jnp.int32), axis=1) // 2
    order = [0, off1, -off1, sign * off2, -sign * off2]
    place = sum(jnp.where(clus == 2 + order[m], m, 0) for m in range(1, 5))
    code = jnp.where(inside, place * used + rank, -1)
    unknowns = 5 * used
    spread = (lax.broadcasted_iota(jnp.int32, (unknowns, 7 * cons), 0) == code[None, :]).astype(BF16)
    nbr_code = jnp.where(want_a, code[cons : 2 * cons], code[2 * cons : 3 * cons])
    pair_code = jnp.concatenate([code[:cons], nbr_code])
    gather = (pair_code[:, None] == lax.broadcasted_iota(jnp.int32, (2 * cons, unknowns), 1)).astype(BF16)
    weights_nbr = jnp.where(want_a, near_a[:face_len], near_b[:face_len])
    weights_pair = jnp.concatenate([weights, dot(selector, weights_nbr).astype(BF16)], axis=1)

    far = coarse_load.shape[0]
    values_near = jnp.concatenate(
        [
            values,
            cor_a[face_len : face_len + cons],
            cor_b[face_len : face_len + cons],
            far_mine[:cons],
            far_other[:cons],
            far_mine[far:],
            far_other[far:],
        ]
    )
    blocks = jnp.stack(
        [
            used_block,
            cor_a[face_len + cons :],
            cor_b[face_len + cons :],
            far_mine[cons:far],
            far_other[cons:far],
        ]
    )[:, :, :used]
    rhs = dot(spread, values_near).astype(BF16).reshape(5, used, -1)
    coarse = jnp.einsum("quv,qvc->quc", blocks, rhs, preferred_element_type=F32).astype(BF16)
    picked = dot(gather, coarse.reshape(unknowns, -1)).astype(BF16)
    facing = dot(selector, jnp.where(want_a, cor_a[:face_len], cor_b[:face_len]))
    precond = (0.5 * (correction + facing + dot(weights_pair, picked))).astype(BF16)

    precond_all = lax.all_gather(precond, "sec", axis=0, tiled=True)
    image = dot(s_rows, precond_all).astype(BF16)
    return precond[None], image[None]


def solution(mesh):
    placed = (
        P("sub", "sec", None),
        P("sub", "sec", None),
        P("sub", "sec", None),
        P("sub", "sec", None),
        P("sub", "sec", None),
        P("sub", "sec", None),
        P("sub", None),
        P("sub", "sec"),
        P("sub", None),
    )
    return jax.shard_map(
        local,
        mesh=mesh,
        in_specs=placed,
        out_specs=(P("sub", "sec", None), P("sub", "sec", None)),
        check_vma=False,
    )
```

time: 115 us -> 52.2 us (0.45)
  waiting for transfers between devices: 40.9 us -> 6.86 us
  between operations: 14.9 us -> 1.77 us
  starting transfers between devices: 23.8 us -> 16.7 us
  blocking collectives: 24.7 us -> 18.7 us
  local copies, waits for them, and re-layouts: 2.92 us -> 1.5 us
    psum x1 -> x0, waiting for transfers between devices: 33.1 us -> none  [local(): constraint_values = lax.psum(constraint_part, 'sec')]
    ppermute x10, starting transfers between devices: 23.7 us -> 16.7 us  [the longest x6 9.27 us: swap_columns(): lax.ppermute(array, 'sub', [(i, partner(kind, i, count)) for i in range(c...]
    all_gather x4 -> x3, blocking collectives: 24.7 us -> 18.7 us  [the longest x1 6.5 us: local(): iterate = lax.all_gather(solution[0], 'sec', axis=0, tiled=True)]
    scatter-add x1 -> x0, other arithmetic: 2.47 us -> none  [local(): jax.ops.segment_sum(value_near.reshape(-1, col_count), owned_slot, num_se...]
    dot_general x8 -> x12, matrix products: 3.78 us -> 3.55 us  [the longest x10 3.18 us: dot(): return jnp.dot(a, b, preferred_element_type=F32)]
  transfers between devices with their start and end apart: 11 -> 10, of which waited for: 6 -> 4; matrix products, arithmetic and copies ran while one was open for 1% -> 9% of each run, Pallas kernels for 0% -> 0%
where the time goes in v1:
time: 52.2 us; the launch traced here: 52 us
  blocking collectives  18.7 us (36%)
  starting transfers between devices  16.7 us (32%)
  waiting for transfers between devices  6.86 us (13%)
  matrix products  3.55 us (7%)
  other arithmetic  2.93 us (6%)
  between operations  1.77 us (3%)
  local copies, waits for them, and re-layouts  1.5 us (3%)
    ppermute x6, starting transfers between devices, swap_columns(): lax.ppermute(array, 'sub', [(i, partner(kind, i, count)) for i in range(c...  9.27 us
    all_gather x1, blocking collectives, local(): iterate = lax.all_gather(solution[0], 'sec', axis=0, tiled=True)  6.5 us
    all_gather x1, blocking collectives, local(): around = lax.all_gather(packed, 'sec', axis=0)  6.37 us
    ppermute x3, starting transfers between devices, swap_by_section(): return lax.ppermute(array, ('sec', 'sub'), moves)  5.91 us
    all_gather x1, blocking collectives, local(): precond_all = lax.all_gather(precond, 'sec', axis=0, tiled=True)  5.78 us
    ppermute x6, waiting for transfers between devices, swap_columns(): lax.ppermute(array, 'sub', [(i, partner(kind, i, count)) for i in range(c...  4.73 us
    dot_general x10, matrix products, dot(): return jnp.dot(a, b, preferred_element_type=F32)  3.18 us
    ppermute x3, waiting for transfers between devices, swap_by_section(): return lax.ppermute(array, ('sec', 'sub'), moves)  2.13 us
  transfers between devices with their start and end apart: 10, of which 4 were waited for; matrix products, arithmetic and copies ran while one was open for 9% of the time, Pallas kernels for 0%

profile of v1, /device:TPU:0, one launch (start us, length us, event | category | flops | bytes accessed | tf_op | source)
XLA Modules:
  0.0 52.0 jit_solution(424004631807403690)
XLA Ops:
  0.7 0.7 %fusion.84 = (bf16[1,128]{1,0:T(2,128)(2,1)S(1)}, s32[1,128]{1,0:T(1,128)S(1)}) fusion(s32[1,128]{1,0:T(1,128)} %param.17, s32[]{:T(128)S(6)} %axis_index.25), kind=kLoop, calls=%fused_computation.216 | loop fusion | flops 5504 | bytes 1284 | tf_op jit(solution)/shard_map/convert.3
  1.4 3.1 %collective-permute-start.4 = (bf16[16,128]{1,0:T(8,128)(2,1)S(1)}, bf16[16,128]{1,0:T(8,128)(2,1)S(1)}, u32[]{:S(2)}, u32[]{:S(2)}) collective-permute-start(bf16[16,128]{1,0:T(8,128)(2,1)S(1)} %pad.8), channel_id=1, source_target_pairs={{0,2},{1,3},{2,0},{3,1},{4,6},{5,7},{6,4},{7,5},{8,14},{9,15},{10,... | collective-permute-start | bytes 12296 | tf_op jit(solution)/shard_map/ppermute | solution.py:36
  4.6 0.8 %pad_maximum_fusion.2 = bf16[272,128]{1,0:T(8,128)(2,1)S(1)} fusion(bf16[16,128]{1,0:T(8,128)(2,1)S(1)} %pad.8, bf16[256,128]{1,0:T(8,128)(2,1)} %bitcast.261), kind=kLoop, calls=%fused_computation.54 | loop fusion | flops 139264 | bytes 139264 | tf_op jit(solution)/shard_map/concatenate | solution.py:89
  5.4 3.4 %collective-permute-start.3 = (bf16[272,128]{1,0:T(8,128)(2,1)S(1)}, bf16[272,128]{1,0:T(8,128)(2,1)S(1)}, u32[]{:S(2)}, u32[]{:S(2)}) collective-permute-start(bf16[272,128]{1,0:T(8,128)(2,1)S(1)} %pad_maximum_fusion.2), channel_id=1, source_target_pairs={{0,7},{1,2},{2,1},{3,4},{4,3},{5,6},{6,5},{7,0},{8,15},{9,10},{10,... | collective-permute-start | bytes 208904 | tf_op jit(solution)/shard_map/ppermute | solution.py:26
  8.8 6.5 %all-gather = bf16[1,1024,128]{2,1,0:T(8,128)(2,1)S(1)} all-gather(bf16[1,256,128]{2,1,0:T(8,128)(2,1)} %param.13), channel_id=2, replica_groups=mesh['sec'=4,'sub'=8] {'sec'}, dimensions={1}, use_global_device_ids=true | all-gather | bytes 327680 | tf_op jit(solution)/shard_map/all_gather | solution.py:93
  15.4 0.3 fusion.95
  15.7 2.6 %collective-permute-start.1 = (bf16[256,128]{1,0:T(8,128)(2,1)S(1)}, bf16[256,128]{1,0:T(8,128)(2,1)S(1)}, u32[]{:S(2)}, u32[]{:S(2)}) collective-permute-start(bf16[256,128]{1,0:T(8,128)(2,1)S(1)} %get-tuple-element.63), channel_id=1, source_target_pairs={{0,7},{1,2},{2,1},{3,4},{4,3},{5,6},{6,5},{7,0},{8,15},{9,10},{10,... | collective-permute-start | bytes 196616 | tf_op jit(solution)/shard_map/ppermute | solution.py:26
  18.2 0.5 %collective-permute-start = (bf16[256,128]{1,0:T(8,128)(2,1)S(1)}, bf16[256,128]{1,0:T(8,128)(2,1)S(1)}, u32[]{:S(2)}, u32[]{:S(2)}) collective-permute-start(bf16[256,128]{1,0:T(8,128)(2,1)S(1)} %get-tuple-element.63), channel_id=1, source_target_pairs={{0,1},{1,0},{2,3},{3,2},{4,5},{5,4},{6,7},{7,6},{8,9},{9,8},{10,11... | collective-permute-start | bytes 196616 | tf_op jit(solution)/shard_map/ppermute | solution.py:26
  18.9 0.6 %constant_dynamic-slice_fusion = s32[1,1]{1,0:T(1,128)} fusion(s32[1,4]{1,0:T(1,128)S(1)} %copy-done.7, s32[]{:T(128)S(6)} %select_n.297), kind=kLoop, calls=%fused_computation.209 | loop fusion | bytes 12 | tf_op jit(solution)/shard_map/dynamic_slice | solution.py:100
  20.2 2.7 %collective-permute-done.1 = bf16[256,128]{1,0:T(8,128)(2,1)S(1)} collective-permute-done((bf16[256,128]{1,0:T(8,128)(2,1)S(1)}, bf16[256,128]{1,0:T(8,128)(2,1)S(1)}, u32[]{:S(2)}, u32[]{:S(2)}) %collective-permute-start.1) | collective-permute-done | bytes 65568 | tf_op jit(solution)/shard_map/ppermute | solution.py:26
  22.9 0.8 %collective-permute-done = bf16[256,128]{1,0:T(8,128)(2,1)S(1)} collective-permute-done((bf16[256,128]{1,0:T(8,128)(2,1)S(1)}, bf16[256,128]{1,0:T(8,128)(2,1)S(1)}, u32[]{:S(2)}, u32[]{:S(2)}) %collective-permute-start) | collective-permute-done | bytes 65568 | tf_op jit(solution)/shard_map/ppermute | solution.py:26
  23.7 0.2 fusion.7
  24.0 0.2 fusion.10
  24.4 0.2 convert_reduce_fusion.1
  24.7 0.4 fusion.2
  25.1 0.4 fusion.11
  25.5 6.4 %all-gather.1 = bf16[1856,128]{1,0:T(8,128)(2,1)S(1)} all-gather(bf16[464,128]{1,0:T(8,128)(2,1)S(1)} %fusion.31), channel_id=3, replica_groups=mesh['sec'=4,'sub'=8] {'sec'}, dimensions={0}, use_global_device_ids=true | all-gather | bytes 593920 | tf_op jit(solution)/shard_map/all_gather | solution.py:133
  32.0 1.0 %collective-permute-start.8 = (bf16[128,128]{1,0:T(8,128)(2,1)S(1)}, bf16[128,128]{1,0:T(8,128)(2,1)S(1)}, u32[]{:S(2)}, u32[]{:S(2)}) collective-permute-start(bf16[128,128]{1,0:T(8,128)(2,1)S(1)} %slice_reduce_fusion), channel_id=1, source_target_pairs={{0,3},{1,6},{2,5},{3,0},{4,7},{5,2},{6,1},{7,4},{8,13},{9,12},{10,... | collective-permute-start | bytes 98312 | tf_op jit(solution)/shard_map/ppermute | solution.py:36
  33.0 0.3 fusion.96
  33.3 2.7 %collective-permute-start.6 = (bf16[448,128]{1,0:T(8,128)(2,1)S(1)}, bf16[448,128]{1,0:T(8,128)(2,1)S(1)}, u32[]{:S(2)}, u32[]{:S(2)}) collective-permute-start(bf16[448,128]{1,0:T(8,128)(2,1)S(1)} %pad_maximum_fusion), channel_id=1, source_target_pairs={{0,7},{1,2},{2,1},{3,4},{4,3},{5,6},{6,5},{7,0},{8,15},{9,10},{10,... | collective-permute-start | bytes 344072 | tf_op jit(solution)/shard_map/ppermute | solution.py:26
  36.1 0.7 %convert_reduce_fusion = s32[896]{0:T(1024)S(1)} fusion(s32[896]{0:T(1024)S(1)} %get-tuple-element.46, s32[896]{0:T(1024)S(1)} %get-tuple-element.45), kind=kLoop, calls=%fused_computation | loop fusion | flops 4013184 | bytes 10752 | tf_op jit(solution)/shard_map/reduce_sum | solution.py:162
  36.9 1.8 %collective-permute-start.7 = (bf16[192,128]{1,0:T(8,128)(2,1)S(1)}, bf16[192,128]{1,0:T(8,128)(2,1)S(1)}, u32[]{:S(2)}, u32[]{:S(2)}) collective-permute-start(bf16[192,128]{1,0:T(8,128)(2,1)S(1)} %pad_maximum_fusion.3), channel_id=1, source_target_pairs={{0,2},{1,3},{2,0},{3,1},{4,6},{5,7},{6,4},{7,5},{8,14},{9,15},{10,... | collective-permute-start | bytes 147464 | tf_op jit(solution)/shard_map/ppermute | solution.py:36
  38.6 0.2 convolution_convert_fusion.3
  38.9 2.1 %collective-permute-done.7 = bf16[192,128]{1,0:T(8,128)(2,1)S(1)} collective-permute-done((bf16[192,128]{1,0:T(8,128)(2,1)S(1)}, bf16[192,128]{1,0:T(8,128)(2,1)S(1)}, u32[]{:S(2)}, u32[]{:S(2)}) %collective-permute-start.7) | collective-permute-done | bytes 49184 | tf_op jit(solution)/shard_map/ppermute | solution.py:36
  41.0 1.6 %collective-permute-start.9 = (bf16[320,128]{1,0:T(8,128)(2,1)S(1)}, bf16[320,128]{1,0:T(8,128)(2,1)S(1)}, u32[]{:S(2)}, u32[]{:S(2)}) collective-permute-start(bf16[320,128]{1,0:T(8,128)(2,1)S(1)} %pad_maximum_fusion.1), channel_id=1, source_target_pairs={{0,8},{8,0},{16,24},{24,16},{1,9},{9,1},{17,25},{25,17},{2,10},{10... | collective-permute-start | bytes 245768 | tf_op jit(solution)/shard_map/ppermute | solution.py:40
  42.6 1.2 %collective-permute-done.5 = bf16[448,128]{1,0:T(8,128)(2,1)S(1)} collective-permute-done((bf16[448,128]{1,0:T(8,128)(2,1)S(1)}, bf16[448,128]{1,0:T(8,128)(2,1)S(1)}, u32[]{:S(2)}, u32[]{:S(2)}) %collective-permute-start.5) | collective-permute-done | bytes 114720 | tf_op jit(solution)/shard_map/ppermute | solution.py:26
  43.9 0.3 fusion.5
  44.4 0.5 fusion.9
  44.9 0.2 fusion.6
  45.1 5.8 %all_gather.15 = bf16[1024,128]{1,0:T(8,128)(2,1)S(1)} all-gather(bf16[256,128]{1,0:T(8,128)(2,1)S(1)} %fusion.6), channel_id=1, replica_groups=mesh['sec'=4,'sub'=8] {'sec'}, dimensions={0}, use_global_device_ids=true | all-gather | bytes 327680 | tf_op jit(solution)/shard_map/all_gather | solution.py:201
  50.9 0.3 fusion.8
  51.3 0.7 %copy.14 = bf16[1,256,128]{2,1,0:T(8,128)(2,1)} copy(bf16[1,256,128]{1,2,0:T(8,128)(2,1)S(1)} %fusion.8) | data formatting | bytes 131072
  (73 shorter events, 0.8 us)
Async XLA Ops:
  0.6 14.7 %copy-start = (bf16[1,256,1024]{2,1,0:T(8,128)(2,1)S(1)}, bf16[1,256,1024]{2,1,0:T(8,128)(2,1)}, u32[]{:S(2)}) copy-start(bf16[1,256,1024]{2,1,0:T(8,128)(2,1)} %param.9) | copy-start | bytes 1572868
  0.6 14.7 %copy-start.5 = (bf16[1,256,128]{2,1,0:T(8,128)(2,1)S(1)}, bf16[1,256,128]{2,1,0:T(8,128)(2,1)}, u32[]{:S(2)}) copy-start(bf16[1,256,128]{2,1,0:T(8,128)(2,1)} %param.14) | copy-start | bytes 196612
  1.4 24.0 %collective-permute-start.4 = (bf16[16,128]{1,0:T(8,128)(2,1)S(1)}, bf16[16,128]{1,0:T(8,128)(2,1)S(1)}, u32[]{:S(2)}, u32[]{:S(2)}) collective-permute-start(bf16[16,128]{1,0:T(8,128)(2,1)S(1)} %pad.8), channel_id=1, source_target_pairs={{0,2},{1,3},{2,0},{3,1},{4,6},{5,7},{6,4},{7,5},{8,14},{9,15},{10,... | collective-permute-start | bytes 12296 | tf_op jit(solution)/shard_map/ppermute | solution.py:36
  5.4 18.8 %collective-permute-start.3 = (bf16[272,128]{1,0:T(8,128)(2,1)S(1)}, bf16[272,128]{1,0:T(8,128)(2,1)S(1)}, u32[]{:S(2)}, u32[]{:S(2)}) collective-permute-start(bf16[272,128]{1,0:T(8,128)(2,1)S(1)} %pad_maximum_fusion.2), channel_id=1, source_target_pairs={{0,7},{1,2},{2,1},{3,4},{4,3},{5,6},{6,5},{7,0},{8,15},{9,10},{10,... | collective-permute-start | bytes 208904 | tf_op jit(solution)/shard_map/ppermute | solution.py:26
  8.8 15.4 %collective-permute-start.2 = (bf16[272,128]{1,0:T(8,128)(2,1)S(1)}, bf16[272,128]{1,0:T(8,128)(2,1)S(1)}, u32[]{:S(2)}, u32[]{:S(2)}) collective-permute-start(bf16[272,128]{1,0:T(8,128)(2,1)S(1)} %pad_maximum_fusion.2), channel_id=1, source_target_pairs={{0,1},{1,0},{2,3},{3,2},{4,5},{5,4},{6,7},{7,6},{8,9},{9,8},{10,11... | collective-permute-start | bytes 208904 | tf_op jit(solution)/shard_map/ppermute | solution.py:26
  15.3 3.5 %copy-start.7 = (s32[1,4]{1,0:T(1,128)S(1)}, s32[1,4]{1,0:T(1,128)}, u32[]{:S(2)}) copy-start(s32[1,4]{1,0:T(1,128)} %param.15) | copy-start | bytes 52
  15.4 8.4 %copy-start.6 = (s32[1,256]{1,0:T(1,128)S(1)}, s32[1,256]{1,0:T(1,128)}, u32[]{:S(2)}) copy-start(s32[1,256]{1,0:T(1,128)} %param.16) | copy-start | bytes 3076
  15.4 8.6 %copy-start.3 = (bf16[1,256,128]{2,1,0:T(8,128)(2,1)S(1)}, bf16[1,256,128]{2,1,0:T(8,128)(2,1)}, u32[]{:S(2)}) copy-start(bf16[1,256,128]{2,1,0:T(8,128)(2,1)} %param.11) | copy-start | bytes 196612
  15.7 7.2 %collective-permute-start.1 = (bf16[256,128]{1,0:T(8,128)(2,1)S(1)}, bf16[256,128]{1,0:T(8,128)(2,1)S(1)}, u32[]{:S(2)}, u32[]{:S(2)}) collective-permute-start(bf16[256,128]{1,0:T(8,128)(2,1)S(1)} %get-tuple-element.63), channel_id=1, source_target_pairs={{0,7},{1,2},{2,1},{3,4},{4,3},{5,6},{6,5},{7,0},{8,15},{9,10},{10,... | collective-permute-start | bytes 196616 | tf_op jit(solution)/shard_map/ppermute | solution.py:26
  18.2 5.5 %collective-permute-start = (bf16[256,128]{1,0:T(8,128)(2,1)S(1)}, bf16[256,128]{1,0:T(8,128)(2,1)S(1)}, u32[]{:S(2)}, u32[]{:S(2)}) collective-permute-start(bf16[256,128]{1,0:T(8,128)(2,1)S(1)} %get-tuple-element.63), channel_id=1, source_target_pairs={{0,1},{1,0},{2,3},{3,2},{4,5},{5,4},{6,7},{7,6},{8,9},{9,8},{10,11... | collective-permute-start | bytes 196616 | tf_op jit(solution)/shard_map/ppermute | solution.py:26
  20.1 4.9 %copy-start.2 = (bf16[1,192,768]{2,1,0:T(8,128)(2,1)S(1)}, bf16[1,192,768]{2,1,0:T(8,128)(2,1)}, u32[]{:S(2)}) copy-start(bf16[1,192,768]{2,1,0:T(8,128)(2,1)} %param.12) | copy-start | bytes 884740
  31.9 1.1 %copy-start.1 = (bf16[1,256,1024]{2,1,0:T(8,128)(2,1)S(1)}, bf16[1,256,1024]{2,1,0:T(8,128)(2,1)}, u32[]{:S(2)}) copy-start(bf16[1,256,1024]{2,1,0:T(8,128)(2,1)} %param.10) | copy-start | bytes 1572868
  32.0 7.0 %collective-permute-start.8 = (bf16[128,128]{1,0:T(8,128)(2,1)S(1)}, bf16[128,128]{1,0:T(8,128)(2,1)S(1)}, u32[]{:S(2)}, u32[]{:S(2)}) collective-permute-start(bf16[128,128]{1,0:T(8,128)(2,1)S(1)} %slice_reduce_fusion), channel_id=1, source_target_pairs={{0,3},{1,6},{2,5},{3,0},{4,7},{5,2},{6,1},{7,4},{8,13},{9,12},{10,... | collective-permute-start | bytes 98312 | tf_op jit(solution)/shard_map/ppermute | solution.py:36
  33.3 10.5 %collective-permute-start.6 = (bf16[448,128]{1,0:T(8,128)(2,1)S(1)}, bf16[448,128]{1,0:T(8,128)(2,1)S(1)}, u32[]{:S(2)}, u32[]{:S(2)}) collective-permute-start(bf16[448,128]{1,0:T(8,128)(2,1)S(1)} %pad_maximum_fusion), channel_id=1, source_target_pairs={{0,7},{1,2},{2,1},{3,4},{4,3},{5,6},{6,5},{7,0},{8,15},{9,10},{10,... | collective-permute-start | bytes 344072 | tf_op jit(solution)/shard_map/ppermute | solution.py:26
  36.0 7.8 %collective-permute-start.5 = (bf16[448,128]{1,0:T(8,128)(2,1)S(1)}, bf16[448,128]{1,0:T(8,128)(2,1)S(1)}, u32[]{:S(2)}, u32[]{:S(2)}) collective-permute-start(bf16[448,128]{1,0:T(8,128)(2,1)S(1)} %pad_maximum_fusion), channel_id=1, source_target_pairs={{0,1},{1,0},{2,3},{3,2},{4,5},{5,4},{6,7},{7,6},{8,9},{9,8},{10,11... | collective-permute-start | bytes 344072 | tf_op jit(solution)/shard_map/ppermute | solution.py:26
  36.9 4.2 %collective-permute-start.7 = (bf16[192,128]{1,0:T(8,128)(2,1)S(1)}, bf16[192,128]{1,0:T(8,128)(2,1)S(1)}, u32[]{:S(2)}, u32[]{:S(2)}) collective-permute-start(bf16[192,128]{1,0:T(8,128)(2,1)S(1)} %pad_maximum_fusion.3), channel_id=1, source_target_pairs={{0,2},{1,3},{2,0},{3,1},{4,6},{5,7},{6,4},{7,5},{8,14},{9,15},{10,... | collective-permute-start | bytes 147464 | tf_op jit(solution)/shard_map/ppermute | solution.py:36
  41.0 2.8 %collective-permute-start.9 = (bf16[320,128]{1,0:T(8,128)(2,1)S(1)}, bf16[320,128]{1,0:T(8,128)(2,1)S(1)}, u32[]{:S(2)}, u32[]{:S(2)}) collective-permute-start(bf16[320,128]{1,0:T(8,128)(2,1)S(1)} %pad_maximum_fusion.1), channel_id=1, source_target_pairs={{0,8},{8,0},{16,24},{24,16},{1,9},{9,1},{17,25},{25,17},{2,10},{10... | collective-permute-start | bytes 245768 | tf_op jit(solution)/shard_map/ppermute | solution.py:40
  45.1 6.1 %copy-start.4 = (bf16[256,128]{1,0:T(8,128)(2,1)}, bf16[256,128]{1,0:T(8,128)(2,1)S(1)}, u32[]{:S(2)}) copy-start(bf16[256,128]{1,0:T(8,128)(2,1)S(1)} %fusion.6) | copy-start | bytes 196612

commit v2 on v1

--- a/solution.py
+++ b/solution.py
@@ -1,7 +1,10 @@
 import jax
 import jax.numpy as jnp
 from jax import lax
+from jax.experimental import pallas as pl
+from jax.experimental.pallas import tpu as pltpu
 from jax.sharding import PartitionSpec as P
+
 
 F32 = jnp.float32
 BF16 = jnp.bfloat16
@@ -38,6 +41,45 @@
 
 def swap_cores(array):
     return lax.ppermute(array, "sec", [(i, i ^ 1) for i in range(lax.axis_size("sec"))])
+
+
+def swap_chips(array):
+    return lax.ppermute(array, "sec", [(i, i ^ 2) for i in range(lax.axis_size("sec"))])
+
+
+def fetch_kernel(*refs):
+    arrays = (len(refs) - 2) // 2
+    sems = refs[-1]
+    copies = [
+        pltpu.make_async_copy(refs[k], refs[arrays + k], sems.at[k]) for k in range(arrays)
+    ]
+    for copy in copies:
+        copy.start()
+    for copy in copies:
+        copy.wait()
+    glued = refs[2 * arrays]
+    table = refs[arrays][...]
+    section = lax.axis_index("sec")
+    place = lax.broadcasted_iota(jnp.int32, table.shape, 1)
+    for row, face in enumerate((section, section ^ 2)):
+        glued[row : row + 1, :] = jnp.zeros((1, glued.shape[1]), jnp.int32) + jnp.sum(
+            jnp.where(place == face, table, 0), axis=1, keepdims=True
+        )
+
+
+def fetch(*arrays):
+    return pl.pallas_call(
+        fetch_kernel,
+        out_shape=[pltpu.VMEM(a.shape, a.dtype) for a in arrays] + [pltpu.VMEM((2, 128), jnp.int32)],
+        in_specs=[pl.BlockSpec(memory_space=pl.ANY)] * len(arrays),
+        out_specs=[pl.BlockSpec(memory_space=pltpu.VMEM)] * (len(arrays) + 1),
+        scratch_shapes=[pltpu.SemaphoreType.DMA((len(arrays),))],
+        name="fetch",
+    )(*arrays)
+
+
+def one_hot(index, length):
+    return (index[:, None] == lax.broadcasted_iota(jnp.int32, (index.shape[0], length), 1)).astype(BF16)
 
 
 def dot(a, b):
@@ -83,47 +125,65 @@
     off1 = jnp.where(even, 1, -1)
     off2 = jnp.where(column % 4 < 2, 2, -2)
     off3 = jnp.where(even, 3, -3)
-
-    own_code = encode_dof(coarse_dof[0], column, count, coarse_len)
-    far_code = swap_by_section(own_code, KINDS)
+    dec = lambda rows, off: decode_dof(rows, off, coarse_len)
+
+    def by_chip(own, peer):
+        low = section // 2 == 0
+        return jnp.concatenate([jnp.where(low, own, peer), jnp.where(low, peer, own)])
+
+    def by_core(mine, other):
+        even_core = jnp.where(core == 0, mine, other)
+        odd_core = jnp.where(core == 0, other, mine)
+        pieces = [even_core[:face_len], odd_core[:face_len], even_core[face_len:], odd_core[face_len:]]
+        return jnp.concatenate(pieces)
+
+    iterate_peer = swap_chips(solution[0])
+    n_peer = swap_chips(n_rows)
+    _, weights, own_dof, face_index, load_rows, iterate_own, n_own, glued = fetch(
+        neighbours, weights, coarse_dof, face_index, load[0], solution[0], n_rows
+    )
+    own_code = encode_dof(own_dof[0], column, count, coarse_len)
     first = jnp.concatenate([weights, own_code])
     near_b = swap_columns(first, "B")
     near_a = swap_columns(first, "A")
-
-    iterate = lax.all_gather(solution[0], "sec", axis=0, tiled=True)
-    residual = load[0].astype(F32) - dot(s_rows, iterate)
+    iterate_other = swap_cores(solution[0])
+    iterate_both = swap_cores(iterate_peer)
+    iterate = by_core(by_chip(iterate_own, iterate_peer), by_chip(iterate_other, iterate_both))
+    residual = load_rows.astype(F32) - dot(s_rows, iterate)
 
     residual_half = residual.astype(BF16)
     res_b = swap_columns(residual_half, "B")
     res_a = swap_columns(residual_half, "A")
-
-    nbr = neighbours[0, section]
-    want_a = ((nbr - column - off1) % count) == 0
-    positions = lax.broadcasted_iota(jnp.int32, (face_len, face_len), 1)
-    selector = (face_index[0][:, None] == positions).astype(BF16)
-
-    dec = lambda rows, off: decode_dof(rows, off, coarse_len)
-    parts3 = [
-        dec(own_code, 0),
-        dec(near_a[face_len:], off1),
-        dec(near_b[face_len:], -off1),
-    ]
+    far_code = swap_by_section(own_code, KINDS)
+
+    from_a = ((glued - column - off1) % count) == 0
+
+    def wants_a(part, rows, width):
+        return jnp.broadcast_to(from_a[part : part + 1, :width], (rows, width))
+
+    selector = one_hot(face_index[0], face_len)
+
+    own_place = dec(own_code, 0)
+    parts3 = [own_place, dec(near_a[face_len:], off1), dec(near_b[face_len:], -off1)]
     clus3 = jnp.concatenate([p[0] for p in parts3])
     slot3 = jnp.concatenate([p[1] for p in parts3])
     key3 = jnp.where(clus3 == 2, slot3, -1)
     less = (key3[None, :] >= 0) & (key3[None, :] < key3[:, None])
     rank3 = jnp.where(key3 >= 0, jnp.sum(less.astype(jnp.int32), axis=1) // 2, -1)
     by_rank = (lax.broadcasted_iota(jnp.int32, (used, 3 * cons), 0) == rank3[None, :]).astype(BF16)
-    by_slot = (key3[:, None] == lax.broadcasted_iota(jnp.int32, (3 * cons, coarse_len), 1)).astype(BF16)
+    by_slot = one_hot(key3, coarse_len)
     pick_used = dot(by_rank, by_slot).astype(BF16)
-    used_cols = lax.dot_general(
-        c_rows, pick_used, (((1,), (1,)), ((), ())), preferred_element_type=F32
-    ).astype(BF16)
+    used_cols = lax.dot_general(c_rows, pick_used, (((1,), (1,)), ((), ())), preferred_element_type=F32).astype(BF16)
     pick_rows = lax.dynamic_slice_in_dim(pick_used, section * coarse_part, coarse_part, axis=1)
     used_part = (0.25 * dot(pick_rows, used_cols)).astype(BF16)
     used_part = jnp.pad(used_part, ((0, 0), (0, cons - used)))
 
-    matched = jnp.where(want_a, res_a, res_b)
+    weights_nbr = jnp.where(wants_a(0, face_len, cons), near_a[:face_len], near_b[:face_len])
+    face_rows = jnp.pad(face_index.reshape(-1, cons).astype(BF16), ((0, 16 - face_len // cons), (0, 0)))
+    weights_two = jnp.concatenate([weights, dot(selector, weights_nbr).astype(BF16), face_rows])
+    weights_two_peer = swap_chips(weights_two)
+
+    matched = jnp.where(wants_a(0, face_len, 128), res_a, res_b)
     assembled = (residual + dot(selector, matched)).astype(BF16)
     values_part = lax.dot_general(
         weights, assembled, (((0,), (0,)), ((), ())), preferred_element_type=F32
@@ -136,12 +196,12 @@
     at = face_len + cons
     used_block = jnp.sum(around[:, at : at + used].astype(F32), axis=0).astype(BF16)
     far_codes = around[:, at + used :]
-    correction = dot(n_rows, assembled_all)
 
     coarse_load = jnp.concatenate([values, used_block])
+    far3_mine = swap_by_section(values, KINDS[2:])
+    far2_mine = swap_by_section(coarse_load, KINDS[:2])
+    correction = jnp.concatenate([dot(n_own, assembled_all), dot(n_peer, assembled_all)])
     out = jnp.concatenate([correction.astype(BF16), coarse_load])
-    far2_mine = swap_by_section(coarse_load, KINDS[:2])
-    far3_mine = swap_by_section(values, KINDS[2:])
     cor_b = swap_columns(out, "B")
     cor_a = swap_columns(out, "A")
     far_mine = jnp.concatenate([far2_mine, far3_mine])
@@ -165,18 +225,14 @@
     code = jnp.where(inside, place * used + rank, -1)
     unknowns = 5 * used
     spread = (lax.broadcasted_iota(jnp.int32, (unknowns, 7 * cons), 0) == code[None, :]).astype(BF16)
-    nbr_code = jnp.where(want_a, code[cons : 2 * cons], code[2 * cons : 3 * cons])
-    pair_code = jnp.concatenate([code[:cons], nbr_code])
-    gather = (pair_code[:, None] == lax.broadcasted_iota(jnp.int32, (2 * cons, unknowns), 1)).astype(BF16)
-    weights_nbr = jnp.where(want_a, near_a[:face_len], near_b[:face_len])
-    weights_pair = jnp.concatenate([weights, dot(selector, weights_nbr).astype(BF16)], axis=1)
-
+
+    two = 2 * face_len
     far = coarse_load.shape[0]
     values_near = jnp.concatenate(
         [
             values,
-            cor_a[face_len : face_len + cons],
-            cor_b[face_len : face_len + cons],
+            cor_a[two : two + cons],
+            cor_b[two : two + cons],
             far_mine[:cons],
             far_other[:cons],
             far_mine[far:],
@@ -186,20 +242,34 @@
     blocks = jnp.stack(
         [
             used_block,
-            cor_a[face_len + cons :],
-            cor_b[face_len + cons :],
+            cor_a[two + cons :],
+            cor_b[two + cons :],
             far_mine[cons:far],
             far_other[cons:far],
         ]
     )[:, :, :used]
     rhs = dot(spread, values_near).astype(BF16).reshape(5, used, -1)
     coarse = jnp.einsum("quv,qvc->quc", blocks, rhs, preferred_element_type=F32).astype(BF16)
-    picked = dot(gather, coarse.reshape(unknowns, -1)).astype(BF16)
-    facing = dot(selector, jnp.where(want_a, cor_a[:face_len], cor_b[:face_len]))
-    precond = (0.5 * (correction + facing + dot(weights_pair, picked))).astype(BF16)
-
-    precond_all = lax.all_gather(precond, "sec", axis=0, tiled=True)
-    image = dot(s_rows, precond_all).astype(BF16)
+    coarse = coarse.reshape(unknowns, -1)
+
+    def finish(part, select, rows):
+        first_row = part * face_len
+        near = jnp.where(
+            wants_a(part, face_len, 128), cor_a[first_row : first_row + face_len], cor_b[first_row : first_row + face_len]
+        )
+        nbr_code = jnp.where(from_a[part, :cons], code[cons : 2 * cons], code[2 * cons : 3 * cons])
+        pick = one_hot(jnp.concatenate([code[:cons], nbr_code]), unknowns)
+        both = jnp.concatenate([rows[:face_len], rows[face_len:two]], axis=1)
+        added = dot(both, dot(pick, coarse).astype(BF16))
+        return (0.5 * (correction[first_row : first_row + face_len] + dot(select, near) + added)).astype(BF16)
+
+    face_peer = weights_two_peer[two : two + face_len // cons].astype(F32).astype(jnp.int32).reshape(-1)
+    precond = finish(0, selector, weights_two)
+    precond_peer = finish(1, one_hot(face_peer, face_len), weights_two_peer)
+
+    precond_two = by_chip(precond, precond_peer)
+    precond_other = swap_cores(precond_two)
+    image = dot(s_rows, by_core(precond_two, precond_other)).astype(BF16)
     return precond[None], image[None]
 
 

time: 52.2 us -> 56.1 us (1.075)
  blocking collectives: 18.7 us -> 7.27 us
  waiting for transfers between devices: 6.86 us -> 18 us
  starting transfers between devices: 16.7 us -> 20.5 us
  Pallas kernels: 0 us -> 1.84 us
  other arithmetic: 2.93 us -> 1.59 us
  matrix products: 3.55 us -> 4.51 us
  between operations: 1.77 us -> 1.2 us
    all_gather x2 -> x0, blocking collectives: 12.3 us -> none  [the longest x1 6.5 us: local(): iterate = lax.all_gather(solution[0], 'sec', axis=0, tiled=True)]
    ppermute x6, waiting for transfers between devices: 4.73 us -> 11.7 us  [swap_columns(): lax.ppermute(array, 'sub', [(i, partner(kind, i, count)) for i in range(c...]
    ppermute x6, starting transfers between devices: 9.27 us -> 13.7 us  [swap_columns(): lax.ppermute(array, 'sub', [(i, partner(kind, i, count)) for i in range(c...]
    ppermute x0 -> x3, starting transfers between devices: none -> 4.09 us  [swap_chips(): lax.ppermute(array, 'sec', [(i, i ^ 2) for i in range(lax.axis_size('sec'...]
    ppermute x3, starting transfers between devices: 5.91 us -> 2.58 us  [swap_by_section(): return lax.ppermute(array, ('sec', 'sub'), moves)]
    ppermute x0 -> x3, waiting for transfers between devices: none -> 2.63 us  [swap_chips(): lax.ppermute(array, 'sec', [(i, i ^ 2) for i in range(lax.axis_size('sec'...]
    pallas_call x0 -> x1, Pallas kernels: none -> 1.84 us  [fetch(): pl.pallas_call(fetch_kernel, out_shape=[pltpu.VMEM(a.shape, a.dtype) for...]
    ppermute x1 -> x4, starting transfers between devices: 1.56 us -> 0.15 us  [swap_cores(): lax.ppermute(array, 'sec', [(i, i ^ 1) for i in range(lax.axis_size('sec'...]
  transfers between devices with their start and end apart: 10 -> 16, of which waited for: 4 -> 7; matrix products, arithmetic and copies ran while one was open for 9% -> 7% of each run, Pallas kernels for 0% -> 0%
where the time goes in v2:
time: 56.1 us; the launch traced here: 55.9 us
  starting transfers between devices  20.5 us (37%)
  waiting for transfers between devices  18 us (32%)
  blocking collectives  7.27 us (13%)
  matrix products  4.51 us (8%)
  Pallas kernels  1.84 us (3%)
  other arithmetic  1.59 us (3%)
  between operations  1.2 us (2%)
  local copies, waits for them, and re-layouts  0.96 us (2%)
    ppermute x6, starting transfers between devices, swap_columns(): lax.ppermute(array, 'sub', [(i, partner(kind, i, count)) for i in range(c...  13.7 us
    ppermute x6, waiting for transfers between devices, swap_columns(): lax.ppermute(array, 'sub', [(i, partner(kind, i, count)) for i in range(c...  11.7 us
    all_gather x1, blocking collectives, local(): around = lax.all_gather(packed, 'sec', axis=0)  7.27 us
    dot_general x13, matrix products, dot(): return jnp.dot(a, b, preferred_element_type=F32)  4.16 us
    ppermute x3, starting transfers between devices, swap_chips(): lax.ppermute(array, 'sec', [(i, i ^ 2) for i in range(lax.axis_size('sec'...  4.09 us
    ppermute x3, waiting for transfers between devices, swap_chips(): lax.ppermute(array, 'sec', [(i, i ^ 2) for i in range(lax.axis_size('sec'...  2.63 us
    ppermute x3, starting transfers between devices, swap_by_section(): return lax.ppermute(array, ('sec', 'sub'), moves)  2.58 us
    ppermute x3, waiting for transfers between devices, swap_by_section(): return lax.ppermute(array, ('sec', 'sub'), moves)  2.35 us
  transfers between devices with their start and end apart: 16, of which 7 were waited for; matrix products, arithmetic and copies ran while one was open for 7% of the time, Pallas kernels for 0%

profile of v2, /device:TPU:0, one launch (start us, length us, event | category | flops | bytes accessed | tf_op | source)
XLA Modules:
  0.0 55.9 jit_solution(12345762192502878254)
XLA Ops:
  0.7 1.8 %fetch.1 = (s32[1,4]{1,0:T(1,128)}, bf16[256,128]{1,0:T(8,128)(2,1)S(1)}, s32[1,128]{1,0:T(1,128)S(1)}, s32[1,256]{1,0:T(1,128)S(1)}, bf16[256,128]{1,0:T(8,128)...) custom-call(s32[1,4]{1,0:T(1,128)} %refs_0_.1, ...), custom_call_target="tpu_custom_call" | custom-call | tf_op jit(solution)/shard_map/fetch/pallas_call | solution.py:71
  2.6 3.1 %collective-permute-start.5 = (bf16[272,128]{1,0:T(8,128)(2,1)S(1)}, bf16[272,128]{1,0:T(8,128)(2,1)S(1)}, u32[]{:S(2)}, u32[]{:S(2)}) collective-permute-start(bf16[272,128]{1,0:T(8,128)(2,1)S(1)} %pad_maximum_fusion.5), channel_id=1, source_target_pairs={{0,1},{1,0},{2,3},{3,2},{4,5},{5,4},{6,7},{7,6},{8,9},{9,8},{10,11... | collective-permute-start | bytes 208904 | tf_op jit(solution)/shard_map/ppermute | solution.py:29
  5.7 3.5 %collective-permute-start.6 = (bf16[272,128]{1,0:T(8,128)(2,1)S(1)}, bf16[272,128]{1,0:T(8,128)(2,1)S(1)}, u32[]{:S(2)}, u32[]{:S(2)}) collective-permute-start(bf16[272,128]{1,0:T(8,128)(2,1)S(1)} %pad_maximum_fusion.5), channel_id=1, source_target_pairs={{0,7},{1,2},{2,1},{3,4},{4,3},{5,6},{6,5},{7,0},{8,15},{9,10},{10,... | collective-permute-start | bytes 208904 | tf_op jit(solution)/shard_map/ppermute | solution.py:29
  9.2 2.0 %collective-permute-start = (bf16[256,128]{1,0:T(8,128)(2,1)S(1)}, bf16[256,128]{1,0:T(8,128)(2,1)S(1)}, u32[]{:S(2)}, u32[]{:S(2)}) collective-permute-start(bf16[256,128]{1,0:T(8,128)(2,1)S(1)} %bitcast.279), channel_id=1, source_target_pairs={{0,16},{8,24},{16,0},{24,8},{1,17},{9,25},{17,1},{25,9},{2,18},{10... | collective-permute-start | bytes 196616 | tf_op jit(solution)/shard_map/ppermute | solution.py:47
  11.4 2.6 %collective-permute-done = bf16[256,128]{1,0:T(8,128)(2,1)S(1)} collective-permute-done((bf16[256,128]{1,0:T(8,128)(2,1)S(1)}, bf16[256,128]{1,0:T(8,128)(2,1)S(1)}, u32[]{:S(2)}, u32[]{:S(2)}) %collective-permute-start) | collective-permute-done | bytes 65568 | tf_op jit(solution)/shard_map/ppermute | solution.py:47
  14.0 1.7 %collective-permute-start.8 = (bf16[256,1024]{1,0:T(8,128)(2,1)S(1)}, bf16[256,1024]{1,0:T(8,128)(2,1)S(1)}, u32[]{:S(2)}, u32[]{:S(2)}) collective-permute-start(bf16[256,1024]{1,0:T(8,128)(2,1)S(1)} %bitcast.270), channel_id=1, source_target_pairs={{0,16},{8,24},{16,0},{24,8},{1,17},{9,25},{17,1},{25,9},{2,18},{10... | collective-permute-start | bytes 1572872 | tf_op jit(solution)/shard_map/ppermute | solution.py:47
  16.3 0.4 fusion.2
  16.7 0.2 convolution_convert_fusion.4
  17.0 0.3 collective-permute-start.14
  17.5 0.3 fusion.127
  17.8 1.5 %collective-permute-start.3 = (bf16[256,128]{1,0:T(8,128)(2,1)S(1)}, bf16[256,128]{1,0:T(8,128)(2,1)S(1)}, u32[]{:S(2)}, u32[]{:S(2)}) collective-permute-start(bf16[256,128]{1,0:T(8,128)(2,1)S(1)} %get-tuple-element.102), channel_id=1, source_target_pairs={{0,1},{1,0},{2,3},{3,2},{4,5},{5,4},{6,7},{7,6},{8,9},{9,8},{10,11... | collective-permute-start | bytes 196616 | tf_op jit(solution)/shard_map/ppermute | solution.py:29
  19.2 2.4 %collective-permute-start.4 = (bf16[256,128]{1,0:T(8,128)(2,1)S(1)}, bf16[256,128]{1,0:T(8,128)(2,1)S(1)}, u32[]{:S(2)}, u32[]{:S(2)}) collective-permute-start(bf16[256,128]{1,0:T(8,128)(2,1)S(1)} %get-tuple-element.102), channel_id=1, source_target_pairs={{0,7},{1,2},{2,1},{3,4},{4,3},{5,6},{6,5},{7,0},{8,15},{9,10},{10,... | collective-permute-start | bytes 196616 | tf_op jit(solution)/shard_map/ppermute | solution.py:29
  21.6 0.4 fusion.13
  22.1 4.1 %collective-permute-done.4 = bf16[256,128]{1,0:T(8,128)(2,1)S(1)} collective-permute-done((bf16[256,128]{1,0:T(8,128)(2,1)S(1)}, bf16[256,128]{1,0:T(8,128)(2,1)S(1)}, u32[]{:S(2)}, u32[]{:S(2)}) %collective-permute-start.4) | collective-permute-done | bytes 65568 | tf_op jit(solution)/shard_map/ppermute | solution.py:29
  26.7 7.3 %all-gather = bf16[1856,128]{1,0:T(8,128)(2,1)S(1)} all-gather(bf16[464,128]{1,0:T(8,128)(2,1)S(1)} %fusion.53), channel_id=2, replica_groups=mesh['sec'=4,'sub'=8] {'sec'}, dimensions={0}, use_global_device_ids=true | all-gather | bytes 593920 | tf_op jit(solution)/shard_map/all_gather | solution.py:193
  34.0 2.6 %collective-permute-start.12 = (bf16[128,128]{1,0:T(8,128)(2,1)S(1)}, bf16[128,128]{1,0:T(8,128)(2,1)S(1)}, u32[]{:S(2)}, u32[]{:S(2)}) collective-permute-start(bf16[128,128]{1,0:T(8,128)(2,1)S(1)} %slice_reduce_fusion), channel_id=1, source_target_pairs={{0,3},{1,6},{2,5},{3,0},{4,7},{5,2},{6,1},{7,4},{8,13},{9,12},{10,... | collective-permute-start | bytes 98312 | tf_op jit(solution)/shard_map/ppermute | solution.py:39
  36.6 0.3 fusion.129
  37.0 0.7 %convert_reduce_fusion = s32[896]{0:T(1024)S(1)} fusion(s32[896]{0:T(1024)S(1)} %get-tuple-element.81, s32[896]{0:T(1024)S(1)} %get-tuple-element.80), kind=kLoop, calls=%fused_computation | loop fusion | flops 4013184 | bytes 10752 | tf_op jit(solution)/shard_map/reduce_sum | solution.py:222
  37.8 0.3 fusion.128
  38.2 1.1 %collective-permute-start.9 = (bf16[704,128]{1,0:T(8,128)(2,1)S(1)}, bf16[704,128]{1,0:T(8,128)(2,1)S(1)}, u32[]{:S(2)}, u32[]{:S(2)}) collective-permute-start(bf16[704,128]{1,0:T(8,128)(2,1)S(1)} %pad_maximum_fusion), channel_id=1, source_target_pairs={{0,1},{1,0},{2,3},{3,2},{4,5},{5,4},{6,7},{7,6},{8,9},{9,8},{10,11... | collective-permute-start | bytes 540680 | tf_op jit(solution)/shard_map/ppermute | solution.py:29
  39.2 2.3 %collective-permute-done.11 = bf16[192,128]{1,0:T(8,128)(2,1)S(1)} collective-permute-done((bf16[192,128]{1,0:T(8,128)(2,1)S(1)}, bf16[192,128]{1,0:T(8,128)(2,1)S(1)}, u32[]{:S(2)}, u32[]{:S(2)}) %collective-permute-start.11) | collective-permute-done | bytes 49184 | tf_op jit(solution)/shard_map/ppermute | solution.py:39
  41.6 2.2 %collective-permute-start.10 = (bf16[704,128]{1,0:T(8,128)(2,1)S(1)}, bf16[704,128]{1,0:T(8,128)(2,1)S(1)}, u32[]{:S(2)}, u32[]{:S(2)}) collective-permute-start(bf16[704,128]{1,0:T(8,128)(2,1)S(1)} %pad_maximum_fusion), channel_id=1, source_target_pairs={{0,7},{1,2},{2,1},{3,4},{4,3},{5,6},{6,5},{7,0},{8,15},{9,10},{10,... | collective-permute-start | bytes 540680 | tf_op jit(solution)/shard_map/ppermute | solution.py:29
  43.8 0.7 %collective-permute-done.9 = bf16[704,128]{1,0:T(8,128)(2,1)S(1)} collective-permute-done((bf16[704,128]{1,0:T(8,128)(2,1)S(1)}, bf16[704,128]{1,0:T(8,128)(2,1)S(1)}, u32[]{:S(2)}, u32[]{:S(2)}) %collective-permute-start.9) | collective-permute-done | bytes 180256 | tf_op jit(solution)/shard_map/ppermute | solution.py:29
  44.5 6.8 %collective-permute-done.10 = bf16[704,128]{1,0:T(8,128)(2,1)S(1)} collective-permute-done((bf16[704,128]{1,0:T(8,128)(2,1)S(1)}, bf16[704,128]{1,0:T(8,128)(2,1)S(1)}, u32[]{:S(2)}, u32[]{:S(2)}) %collective-permute-start.10) | collective-permute-done | bytes 180256 | tf_op jit(solution)/shard_map/ppermute | solution.py:29
  51.3 0.3 fusion.7
  51.9 0.2 convolution_add_fusion.2
  52.1 0.5 fusion.9
  52.6 0.5 fusion.12
  53.1 0.2 broadcast_select_fusion.5
  53.4 1.3 %collective-permute-done.15 = bf16[512,128]{1,0:T(8,128)(2,1)S(1)} collective-permute-done((bf16[512,128]{1,0:T(8,128)(2,1)S(1)}, bf16[512,128]{1,0:T(8,128)(2,1)S(1)}, u32[]{:S(2)}, u32[]{:S(2)}) %collective-permute-start.15) | collective-permute-done | bytes 131104 | tf_op jit(solution)/shard_map/ppermute | solution.py:43
  54.8 0.3 fusion.11
  55.2 0.7 %copy.16 = bf16[1,256,128]{2,1,0:T(8,128)(2,1)} copy(bf16[1,256,128]{1,2,0:T(8,128)(2,1)S(1)} %fusion.11) | data formatting | bytes 131072
  (95 shorter events, 2.0 us)
Async XLA Ops:
  0.6 16.8 %copy-start = (bf16[1,256,1024]{2,1,0:T(8,128)(2,1)S(1)}, bf16[1,256,1024]{2,1,0:T(8,128)(2,1)}, u32[]{:S(2)}) copy-start(bf16[1,256,1024]{2,1,0:T(8,128)(2,1)} %param.9) | copy-start | bytes 1572868
  0.6 8.6 %copy-start.4 = (bf16[1,256,128]{2,1,0:T(8,128)(2,1)S(1)}, bf16[1,256,128]{2,1,0:T(8,128)(2,1)}, u32[]{:S(2)}) copy-start(bf16[1,256,128]{2,1,0:T(8,128)(2,1)} %param.13) | copy-start | bytes 196612
  0.7 13.3 %copy-start.1 = (bf16[1,256,1024]{2,1,0:T(8,128)(2,1)S(1)}, bf16[1,256,1024]{2,1,0:T(8,128)(2,1)}, u32[]{:S(2)}) copy-start(bf16[1,256,1024]{2,1,0:T(8,128)(2,1)} %param.10) | copy-start | bytes 1572868
  2.6 13.3 %collective-permute-start.5 = (bf16[272,128]{1,0:T(8,128)(2,1)S(1)}, bf16[272,128]{1,0:T(8,128)(2,1)S(1)}, u32[]{:S(2)}, u32[]{:S(2)}) collective-permute-start(bf16[272,128]{1,0:T(8,128)(2,1)S(1)} %pad_maximum_fusion.5), channel_id=1, source_target_pairs={{0,1},{1,0},{2,3},{3,2},{4,5},{5,4},{6,7},{7,6},{8,9},{9,8},{10,11... | collective-permute-start | bytes 208904 | tf_op jit(solution)/shard_map/ppermute | solution.py:29
  5.7 10.1 %collective-permute-start.6 = (bf16[272,128]{1,0:T(8,128)(2,1)S(1)}, bf16[272,128]{1,0:T(8,128)(2,1)S(1)}, u32[]{:S(2)}, u32[]{:S(2)}) collective-permute-start(bf16[272,128]{1,0:T(8,128)(2,1)S(1)} %pad_maximum_fusion.5), channel_id=1, source_target_pairs={{0,7},{1,2},{2,1},{3,4},{4,3},{5,6},{6,5},{7,0},{8,15},{9,10},{10,... | collective-permute-start | bytes 208904 | tf_op jit(solution)/shard_map/ppermute | solution.py:29
  9.2 17.4 %collective-permute-start.7 = (bf16[16,128]{1,0:T(8,128)(2,1)S(1)}, bf16[16,128]{1,0:T(8,128)(2,1)S(1)}, u32[]{:S(2)}, u32[]{:S(2)}) collective-permute-start(bf16[16,128]{1,0:T(8,128)(2,1)S(1)} %pad.11), channel_id=1, source_target_pairs={{0,2},{1,3},{2,0},{3,1},{4,6},{5,7},{6,4},{7,5},{8,14},{9,15},{10,... | collective-permute-start | bytes 12296 | tf_op jit(solution)/shard_map/ppermute | solution.py:39
  9.2 8.1 %collective-permute-start.1 = (bf16[256,128]{1,0:T(8,128)(2,1)S(1)}, bf16[256,128]{1,0:T(8,128)(2,1)S(1)}, u32[]{:S(2)}, u32[]{:S(2)}) collective-permute-start(bf16[256,128]{1,0:T(8,128)(2,1)S(1)} %bitcast.278), channel_id=1, source_target_pairs={{0,8},{8,0},{16,24},{24,16},{1,9},{9,1},{17,25},{25,17},{2,10},{10... | collective-permute-start | bytes 196616 | tf_op jit(solution)/shard_map/ppermute | solution.py:43
  9.2 4.8 %collective-permute-start = (bf16[256,128]{1,0:T(8,128)(2,1)S(1)}, bf16[256,128]{1,0:T(8,128)(2,1)S(1)}, u32[]{:S(2)}, u32[]{:S(2)}) collective-permute-start(bf16[256,128]{1,0:T(8,128)(2,1)S(1)} %bitcast.279), channel_id=1, source_target_pairs={{0,16},{8,24},{16,0},{24,8},{1,17},{9,25},{17,1},{25,9},{2,18},{10... | collective-permute-start | bytes 196616 | tf_op jit(solution)/shard_map/ppermute | solution.py:47
  14.0 23.9 %collective-permute-start.8 = (bf16[256,1024]{1,0:T(8,128)(2,1)S(1)}, bf16[256,1024]{1,0:T(8,128)(2,1)S(1)}, u32[]{:S(2)}, u32[]{:S(2)}) collective-permute-start(bf16[256,1024]{1,0:T(8,128)(2,1)S(1)} %bitcast.270), channel_id=1, source_target_pairs={{0,16},{8,24},{16,0},{24,8},{1,17},{9,25},{17,1},{25,9},{2,18},{10... | collective-permute-start | bytes 1572872 | tf_op jit(solution)/shard_map/ppermute | solution.py:47
  15.8 1.6 %collective-permute-start.2 = (bf16[256,128]{1,0:T(8,128)(2,1)S(1)}, bf16[256,128]{1,0:T(8,128)(2,1)S(1)}, u32[]{:S(2)}, u32[]{:S(2)}) collective-permute-start(bf16[256,128]{1,0:T(8,128)(2,1)S(1)} %collective-permute-done), channel_id=1, source_target_pairs={{0,8},{8,0},{16,24},{24,16},{1,9},{9,1},{17,25},{25,17},{2,10},{10... | collective-permute-start | bytes 196616 | tf_op jit(solution)/shard_map/ppermute | solution.py:43
  17.0 20.8 %collective-permute-start.14 = (bf16[528,128]{1,0:T(8,128)(2,1)S(1)}, bf16[528,128]{1,0:T(8,128)(2,1)S(1)}, u32[]{:S(2)}, u32[]{:S(2)}) collective-permute-start(bf16[528,128]{1,0:T(8,128)(2,1)S(1)} %fusion.41), channel_id=1, source_target_pairs={{0,16},{8,24},{16,0},{24,8},{1,17},{9,25},{17,1},{25,9},{2,18},{10... | collective-permute-start | bytes 405512 | tf_op jit(solution)/shard_map/ppermute | solution.py:47
  17.5 4.2 %copy-start.2 = (bf16[1,192,768]{2,1,0:T(8,128)(2,1)S(1)}, bf16[1,192,768]{2,1,0:T(8,128)(2,1)}, u32[]{:S(2)}) copy-start(bf16[1,192,768]{2,1,0:T(8,128)(2,1)} %param.12) | copy-start | bytes 884740
  17.8 4.3 %collective-permute-start.3 = (bf16[256,128]{1,0:T(8,128)(2,1)S(1)}, bf16[256,128]{1,0:T(8,128)(2,1)S(1)}, u32[]{:S(2)}, u32[]{:S(2)}) collective-permute-start(bf16[256,128]{1,0:T(8,128)(2,1)S(1)} %get-tuple-element.102), channel_id=1, source_target_pairs={{0,1},{1,0},{2,3},{3,2},{4,5},{5,4},{6,7},{7,6},{8,9},{9,8},{10,11... | collective-permute-start | bytes 196616 | tf_op jit(solution)/shard_map/ppermute | solution.py:29
  19.2 7.0 %collective-permute-start.4 = (bf16[256,128]{1,0:T(8,128)(2,1)S(1)}, bf16[256,128]{1,0:T(8,128)(2,1)S(1)}, u32[]{:S(2)}, u32[]{:S(2)}) collective-permute-start(bf16[256,128]{1,0:T(8,128)(2,1)S(1)} %get-tuple-element.102), channel_id=1, source_target_pairs={{0,7},{1,2},{2,1},{3,4},{4,3},{5,6},{6,5},{7,0},{8,15},{9,10},{10,... | collective-permute-start | bytes 196616 | tf_op jit(solution)/shard_map/ppermute | solution.py:29
  34.0 5.2 %collective-permute-start.12 = (bf16[128,128]{1,0:T(8,128)(2,1)S(1)}, bf16[128,128]{1,0:T(8,128)(2,1)S(1)}, u32[]{:S(2)}, u32[]{:S(2)}) collective-permute-start(bf16[128,128]{1,0:T(8,128)(2,1)S(1)} %slice_reduce_fusion), channel_id=1, source_target_pairs={{0,3},{1,6},{2,5},{3,0},{4,7},{5,2},{6,1},{7,4},{8,13},{9,12},{10,... | collective-permute-start | bytes 98312 | tf_op jit(solution)/shard_map/ppermute | solution.py:39
  36.6 5.0 %collective-permute-start.11 = (bf16[192,128]{1,0:T(8,128)(2,1)S(1)}, bf16[192,128]{1,0:T(8,128)(2,1)S(1)}, u32[]{:S(2)}, u32[]{:S(2)}) collective-permute-start(bf16[192,128]{1,0:T(8,128)(2,1)S(1)} %pad_maximum_fusion.6), channel_id=1, source_target_pairs={{0,2},{1,3},{2,0},{3,1},{4,6},{5,7},{6,4},{7,5},{8,14},{9,15},{10,... | collective-permute-start | bytes 147464 | tf_op jit(solution)/shard_map/ppermute | solution.py:39
  38.2 6.3 %collective-permute-start.9 = (bf16[704,128]{1,0:T(8,128)(2,1)S(1)}, bf16[704,128]{1,0:T(8,128)(2,1)S(1)}, u32[]{:S(2)}, u32[]{:S(2)}) collective-permute-start(bf16[704,128]{1,0:T(8,128)(2,1)S(1)} %pad_maximum_fusion), channel_id=1, source_target_pairs={{0,1},{1,0},{2,3},{3,2},{4,5},{5,4},{6,7},{7,6},{8,9},{9,8},{10,11... | collective-permute-start | bytes 540680 | tf_op jit(solution)/shard_map/ppermute | solution.py:29
  41.6 9.7 %collective-permute-start.13 = (bf16[320,128]{1,0:T(8,128)(2,1)S(1)}, bf16[320,128]{1,0:T(8,128)(2,1)S(1)}, u32[]{:S(2)}, u32[]{:S(2)}) collective-permute-start(bf16[320,128]{1,0:T(8,128)(2,1)S(1)} %pad_maximum_fusion.4), channel_id=1, source_target_pairs={{0,8},{8,0},{16,24},{24,16},{1,9},{9,1},{17,25},{25,17},{2,10},{10... | collective-permute-start | bytes 245768 | tf_op jit(solution)/shard_map/ppermute | solution.py:43
  41.6 9.7 %collective-permute-start.10 = (bf16[704,128]{1,0:T(8,128)(2,1)S(1)}, bf16[704,128]{1,0:T(8,128)(2,1)S(1)}, u32[]{:S(2)}, u32[]{:S(2)}) collective-permute-start(bf16[704,128]{1,0:T(8,128)(2,1)S(1)} %pad_maximum_fusion), channel_id=1, source_target_pairs={{0,7},{1,2},{2,1},{3,4},{4,3},{5,6},{6,5},{7,0},{8,15},{9,10},{10,... | collective-permute-start | bytes 540680 | tf_op jit(solution)/shard_map/ppermute | solution.py:29
  52.6 0.7 %copy-start.3 = (bf16[256,128]{1,0:T(8,128)(2,1)}, bf16[256,128]{1,0:T(8,128)(2,1)S(1)}, u32[]{:S(2)}) copy-start(bf16[256,128]{1,0:T(8,128)(2,1)S(1)} %fusion.9) | copy-start | bytes 196612
  53.3 1.4 %collective-permute-start.15 = (bf16[512,128]{1,0:T(8,128)(2,1)S(1)}, bf16[512,128]{1,0:T(8,128)(2,1)S(1)}, u32[]{:S(2)}, u32[]{:S(2)}) collective-permute-start(bf16[512,128]{1,0:T(8,128)(2,1)S(1)} %pad_maximum_fusion.3), channel_id=1, source_target_pairs={{0,8},{8,0},{16,24},{24,16},{1,9},{9,1},{17,25},{25,17},{2,10},{10... | collective-permute-start | bytes 393224 | tf_op jit(solution)/shard_map/ppermute | solution.py:43
